TPU v7x, 128 devices: a whole 4x4x4 slice. The times are simulated.
128 devices in a mesh: row: 16 (over y, z), col: 8 (over x, core).
Axes of the slice: x: 4, y: 4, z: 4, core: 2. Of those that a mesh axis runs over, the one named last changes fastest.
Arguments:
- block_cols: int32 [64, 16], replicated, may hold values from -1 to 63, as said below
- step_dir: bfloat16 [64, 16, 128, 128], P('row', 'col')
- intersection: bfloat16 [64, 16, 128, 128], P('row', 'col')
- density: bfloat16 [64, 16, 128, 128], P('row', 'col')
- kohn_sham: bfloat16 [64, 16, 128, 128], P('row', 'col')
Outputs:
- commutator: bfloat16 [64, 16, 128, 128], P('row', 'col')
- trace_value: float32 [], replicated
Inputs may be any that keep to these rules, and one draw needn't show every extreme that they name: block_cols[i, s] is -1 or a block column of group s // 2, that is from (s // 2) * 8 to (s // 2 + 1) * 8 - 1; the live entries of one block row within one group are distinct; the pattern is symmetric (j is live in row i exactly when i is live in row j) and holds every diagonal block.
All inputs are finite; a program needn't handle non-finite values.
Results may differ from a plain program's by a relative error of at most 0.0057.
Values may be sent and summed in bfloat16 or wider, within the bound.
A program may use at most 64 MiB of HBM per device.

v0:
```python
import jax
import jax.numpy as jnp
from jax import lax
from jax.sharding import PartitionSpec as P


def per_device(block_cols, step_dir, intersection, density, kohn_sham):
    row_total = step_dir.shape[0]
    slot_total = step_dir.shape[1]
    block_size = step_dir.shape[2]
    col_groups = lax.axis_size("col")
    blocks_total = block_cols.shape[0]
    row_index = lax.axis_index("row")
    col_index = lax.axis_index("col")
    own_rows = lax.dynamic_slice_in_dim(block_cols, row_index * row_total, row_total, 0)
    own_cols = lax.dynamic_slice_in_dim(own_rows, col_index * slot_total, slot_total, 1)
    group_cols = lax.dynamic_slice_in_dim(block_cols, col_index * slot_total, slot_total, 1)
    left_live = own_cols >= 0
    targets = own_rows.reshape(row_total, col_groups, slot_total).transpose(1, 0, 2)

    def partial_blocks(left_blocks, gathered, wanted):
        safe_rows = jnp.clip(wanted, 0, blocks_total - 1)
        right_rows = gathered[safe_rows]
        right_cols = group_cols[safe_rows]
        matched = (
            (right_cols[:, :, :, None, :] == own_cols[None, :, None, :, None])
            & left_live[None, :, None, :, None]
            & (wanted >= 0)[:, :, :, None, None]
        )
        picked = jnp.where(
            matched[..., None, None],
            right_rows[:, :, :, None, :, :, :],
            jnp.zeros((), jnp.bfloat16),
        ).sum(axis=4)
        terms = jnp.einsum(
            "iapr,gisaqr->gispq", left_blocks, picked, preferred_element_type=jnp.float32
        )
        group_count = wanted.shape[0]
        return terms.reshape(group_count * row_total, slot_total, block_size, block_size)

    def product(left_blocks, right_blocks):
        gathered = lax.all_gather(right_blocks, "row", axis=0, tiled=True)
        return lax.psum_scatter(
            partial_blocks(left_blocks, gathered, targets), "col", scatter_dimension=0, tiled=True
        )

    scaled_step = product(step_dir, intersection).astype(jnp.bfloat16)
    change = (-(product(scaled_step, density) + product(density, scaled_step))).astype(jnp.bfloat16)
    commutator = (product(kohn_sham, change) - product(change, kohn_sham)).astype(jnp.bfloat16)
    local_trace = jnp.sum(change.astype(jnp.float32) * kohn_sham.astype(jnp.float32))
    trace_value = lax.psum(local_trace, ("row", "col")) / (blocks_total * block_size * block_size)
    return (commutator, trace_value)


def solution(mesh):
    in_specs = (
        P(),
        P("row", "col", None, None),
        P("row", "col", None, None),
        P("row", "col", None, None),
        P("row", "col", None, None),
    )
    out_specs = (P("row", "col", None, None), P())
    return jax.shard_map(
        per_device, mesh=mesh, in_specs=in_specs, out_specs=out_specs, check_vma=False
    )
```

profile of v0, /device:TPU:1, one launch (start us, length us, event | category | flops | bytes accessed | tf_op | source)
XLA Modules:
  0.0 501.8 jit_solution(6847474959793263105)
XLA Ops:
  14.0 50.7 %all-gather.14.cloned.1.call-done = bf16[64,2,128,128]{3,2,1,0:T(8,128)(2,1)} async-done(((bf16[4,2,128,128]{3,2,1,0:T(8,128)(2,1)}), bf16[64,2,128,128]{3,2,1,0:T(8,128)(2,1)}) %all-gather.14.cloned.1.call-update) | async-done | bytes 4194320 | tf_op jit(solution)/shard_map/all_gather | solution.py:42
  64.7 5.2 %gather_fusion.5 = bf16[64,2,128,128]{3,2,1,0:T(8,128)(2,1)} fusion(bf16[64,2,128,128]{3,2,1,0:T(8,128)(2,1)} %all-gather.14.cloned.1.call-done, s32[1024]{0:T(1024)S(1)} %pad_clamp_fusion), kind=kCustom, calls=%fused_computation.5 | custom fusion | bytes 8388864 | tf_op jit(solution)/shard_map/gather | solution.py:23
  69.9 48.0 %all-gather.8.cloned.1.call-done = bf16[64,2,128,128]{3,2,1,0:T(8,128)(2,1)} async-done(((bf16[4,2,128,128]{3,2,1,0:T(8,128)(2,1)}), bf16[64,2,128,128]{3,2,1,0:T(8,128)(2,1)}) %all-gather.8.cloned.1.call-update) | async-done | bytes 4194320 | tf_op jit(solution)/shard_map/all_gather | solution.py:42
  118.0 5.2 %gather_fusion.2 = bf16[64,2,128,128]{3,2,1,0:T(8,128)(2,1)} fusion(bf16[64,2,128,128]{3,2,1,0:T(8,128)(2,1)} %all-gather.8.cloned.1.call-done, s32[1024]{0:T(1024)S(1)} %pad_clamp_fusion), kind=kCustom, calls=%fused_computation.2 | custom fusion | bytes 8388864 | tf_op jit(solution)/shard_map/gather | solution.py:23
  123.2 48.1 %all-gather.6.cloned.1.call-done = bf16[64,2,128,128]{3,2,1,0:T(8,128)(2,1)} async-done(((bf16[4,2,128,128]{3,2,1,0:T(8,128)(2,1)}), bf16[64,2,128,128]{3,2,1,0:T(8,128)(2,1)}) %all-gather.6.cloned.1.call-update) | async-done | bytes 4194320 | tf_op jit(solution)/shard_map/all_gather | solution.py:42
  171.2 5.2 %gather_fusion.1 = bf16[64,2,128,128]{3,2,1,0:T(8,128)(2,1)} fusion(bf16[64,2,128,128]{3,2,1,0:T(8,128)(2,1)} %all-gather.6.cloned.1.call-done, s32[1024]{0:T(1024)S(1)} %pad_clamp_fusion), kind=kCustom, calls=%fused_computation.1 | custom fusion | bytes 8388864 | tf_op jit(solution)/shard_map/gather | solution.py:23
  176.5 17.5 %select_reduce_fusion = (bf16[8,4,2,2,128,128]{5,4,3,2,1,0:T(8,128)(2,1)}, bf16[8,4,2,2,128,128]{5,4,3,2,1,0:T(8,128)(2,1)S(1)}, bf16[8,4,2,2,128,128]{5,4,3,2,1,0:T(8,128)(2,1)}) fusion(pred[8,4,2,2,2]{4,3,2,1,0:T(4,128)(4,1)S(1)} %and_and_fusion, bf16[8,4,2,2,128,128]{5,4,3,2,1,0:T(8,128)(2,1)} %bitcast.70, bf16[8,4,2,2,128,128]{5,4,3,2,1,0:T(8,128)(2,1)} %bitcast.71, ...), kind=kLoop, calls=%fused_computation.6 | loop fusion | flops 18874368 | bytes 25166080 | tf_op jit(solution)/shard_map/reduce_sum | solution.py:34
  193.9 3.2 fusion.11
  197.1 5.4 %copy.48 = f32[8,4,2,128,128]{4,3,2,1,0:T(8,128)} copy(f32[8,4,2,128,128]{3,4,2,0,1:T(8,128)} %fusion.11) | data formatting | bytes 8388608 | tf_op jit(solution)/shard_map/iapr,gisaqr->gispq/transpose | solution.py:35
  202.6 34.9 %reduce-scatter.5.cloned.1.call-done = f32[4,2,128,128]{3,2,1,0:T(8,128)} async-done(((f32[32,2,128,128]{3,2,1,0:T(8,128)}), f32[4,2,128,128]{3,2,1,0:T(8,128)}) %reduce-scatter.5.cloned.1.call-update) | async-done | bytes 524304 | tf_op jit(solution)/shard_map/reduce_scatter | solution.py:43
  239.5 53.7 %all-gather.10.cloned.1.call-done = bf16[64,2,128,128]{3,2,1,0:T(8,128)(2,1)} async-done(((bf16[4,2,128,128]{3,2,1,0:T(8,128)(2,1)}), bf16[64,2,128,128]{3,2,1,0:T(8,128)(2,1)}) %all-gather.10.cloned.1.call-update) | async-done | bytes 4194320 | tf_op jit(solution)/shard_map/all_gather | solution.py:42
  293.2 5.2 %gather_fusion.3 = bf16[64,2,128,128]{3,2,1,0:T(8,128)(2,1)} fusion(bf16[64,2,128,128]{3,2,1,0:T(8,128)(2,1)} %all-gather.10.cloned.1.call-done, s32[1024]{0:T(1024)S(1)} %pad_clamp_fusion), kind=kCustom, calls=%fused_computation.3 | custom fusion | bytes 8388864 | tf_op jit(solution)/shard_map/gather | solution.py:23
  298.4 6.2 %select_reduce_fusion.2 = bf16[8,4,2,2,128,128]{5,4,3,2,1,0:T(8,128)(2,1)S(1)} fusion(pred[8,4,2,2,2]{4,3,2,1,0:T(4,128)(4,1)S(1)} %and_and_fusion, bf16[8,4,2,2,128,128]{5,4,3,2,1,0:T(8,128)(2,1)} %bitcast.69), kind=kLoop, calls=%fused_computation.8 | loop fusion | flops 6291456 | bytes 8388864 | tf_op jit(solution)/shard_map/reduce_sum | solution.py:34
  306.8 3.2 fusion
  310.0 5.4 %copy.51 = f32[8,4,2,128,128]{4,3,2,1,0:T(8,128)} copy(f32[8,4,2,128,128]{3,4,2,0,1:T(8,128)} %fusion) | data formatting | bytes 8388608 | tf_op jit(solution)/shard_map/add | solution.py:48
  315.5 34.8 %reduce-scatter.11.cloned.1.call-done = f32[4,2,128,128]{3,2,1,0:T(8,128)} async-done(((f32[32,2,128,128]{3,2,1,0:T(8,128)}), f32[4,2,128,128]{3,2,1,0:T(8,128)}) %reduce-scatter.11.cloned.1.call-update) | async-done | bytes 524304 | tf_op jit(solution)/shard_map/reduce_scatter | solution.py:43
  352.8 5.4 %fusion.17 = f32[8,4,2,128,128]{3,4,2,0,1:T(8,128)} fusion(bf16[8,4,2,2,128,128]{5,4,3,2,1,0:T(8,128)(2,1)} %get-tuple-element.2, bf16[4,2,128,128]{3,2,1,0:T(8,128)(2,1)} %get-tuple-element.6), kind=kOutput, calls=%fused_computation.25 | convolution fusion | flops 536870912 | bytes 8650752 | tf_op jit(solution)/shard_map/iapr,gisaqr->gispq/dot_general | solution.py:35
  358.2 5.4 %copy.55 = f32[8,4,2,128,128]{4,3,2,1,0:T(8,128)} copy(f32[8,4,2,128,128]{3,4,2,0,1:T(8,128)} %fusion.17) | data formatting | bytes 8388608 | tf_op jit(solution)/shard_map/iapr,gisaqr->gispq/transpose | solution.py:35
  363.6 42.6 %all-gather.12.cloned.1.call-done = bf16[64,2,128,128]{3,2,1,0:T(8,128)(2,1)} async-done(((bf16[4,2,128,128]{3,2,1,0:T(8,128)(2,1)}), bf16[64,2,128,128]{3,2,1,0:T(8,128)(2,1)}) %all-gather.12.cloned.1.call-update) | async-done | bytes 4194320 | tf_op jit(solution)/shard_map/all_gather | solution.py:42
  406.2 5.2 %gather_fusion.4 = bf16[64,2,128,128]{3,2,1,0:T(8,128)(2,1)} fusion(bf16[64,2,128,128]{3,2,1,0:T(8,128)(2,1)} %all-gather.12.cloned.1.call-done, s32[1024]{0:T(1024)S(1)} %pad_clamp_fusion), kind=kCustom, calls=%fused_computation.4 | custom fusion | bytes 8388864 | tf_op jit(solution)/shard_map/gather | solution.py:23
  411.5 6.2 %select_reduce_fusion.1 = bf16[8,4,2,2,128,128]{5,4,3,2,1,0:T(8,128)(2,1)S(1)} fusion(pred[8,4,2,2,2]{4,3,2,1,0:T(4,128)(4,1)S(1)} %and_and_fusion, bf16[8,4,2,2,128,128]{5,4,3,2,1,0:T(8,128)(2,1)} %bitcast.68), kind=kLoop, calls=%fused_computation.7 | loop fusion | flops 6291456 | bytes 8388864 | tf_op jit(solution)/shard_map/reduce_sum | solution.py:34
  417.6 3.2 fusion.14
  420.8 5.5 %copy.53 = f32[8,4,2,128,128]{4,3,2,1,0:T(8,128)} copy(f32[8,4,2,128,128]{3,4,2,0,1:T(8,128)} %fusion.14) | data formatting | bytes 8388608 | tf_op jit(solution)/shard_map/iapr,gisaqr->gispq/transpose | solution.py:35
  426.4 65.1 %psum.7 = f32[]{:T(128)} all-reduce(f32[]{:T(128)} %get-tuple-element.5), channel_id=1, replica_groups=mesh['row'=16,'col'=8] {'row','col'}, use_global_device_ids=true, to_apply=%region_11.12 | all-reduce | flops 1 | bytes 8 | tf_op jit(solution)/shard_map/psum | solution.py:51
  (52 shorter events, 15.6 us)
Async XLA Ops:
  7.2 186.8 %copy-start = (bf16[4,2,128,128]{3,2,1,0:T(8,128)(2,1)S(1)}, bf16[4,2,128,128]{3,2,1,0:T(8,128)(2,1)}, u32[]{:S(2)}) copy-start(bf16[4,2,128,128]{3,2,1,0:T(8,128)(2,1)} %param.6) | copy-start | bytes 786436
  7.2 57.5 %all-gather.14.cloned.1.call-start = ((), (), s32[]{:S(2)}) async-start(), calls=%async_computation.10 | async-start | bytes 4456448 | tf_op jit(solution)/shard_map/all_gather | solution.py:42
  7.9 110.1 %all-gather.8.cloned.1.call-start = ((), (), s32[]{:S(2)}) async-start(), calls=%async_computation.5 | async-start | bytes 4456448 | tf_op jit(solution)/shard_map/all_gather | solution.py:42
  8.7 162.6 %all-gather.6.cloned.1.call-start = ((), (), s32[]{:S(2)}) async-start(), calls=%async_computation.4 | async-start | bytes 4456448 | tf_op jit(solution)/shard_map/all_gather | solution.py:42
  9.4 228.0 %reduce-scatter.5.cloned.1.call-start = ((), (), s32[]{:S(2)}) async-start(), calls=%async_computation.6 | async-start | bytes 4718592 | tf_op jit(solution)/shard_map/reduce_scatter | solution.py:43
  202.5 90.7 %all-gather.10.cloned.1.call-start = ((), (), s32[]{:S(2)}) async-start(), calls=%async_computation.7 | async-start | bytes 4456448 | tf_op jit(solution)/shard_map/all_gather | solution.py:42
  239.2 111.0 %reduce-scatter.11.cloned.1.call-start = ((), (), s32[]{:S(2)}) async-start(), calls=%async_computation.12 | async-start | bytes 4718592 | tf_op jit(solution)/shard_map/reduce_scatter | solution.py:43
  298.4 6.2 %copy-start.4 = (bf16[4,2,128,128]{3,2,1,0:T(8,128)(2,1)S(1)}, bf16[4,2,128,128]{3,2,1,0:T(8,128)(2,1)}, u32[]{:S(2)}) copy-start(bf16[4,2,128,128]{3,2,1,0:T(8,128)(2,1)} %param.8) | copy-start | bytes 786436
  304.6 2.2 copy-start.2
  304.6 2.2 copy-start.3
  315.4 34.9 %copy-start.5 = (bf16[4,2,128,128]{3,2,1,0:T(8,128)(2,1)S(1)}, bf16[4,2,128,128]{3,2,1,0:T(8,128)(2,1)}, u32[]{:S(2)}) copy-start(bf16[4,2,128,128]{3,2,1,0:T(8,128)(2,1)} %param.9) | copy-start | bytes 786436
  315.4 90.8 %all-gather.12.cloned.1.call-start = ((), (), s32[]{:S(2)}) async-start(), calls=%async_computation.8 | async-start | bytes 4456448 | tf_op jit(solution)/shard_map/all_gather | solution.py:42
  352.7 139.4 %reduce-scatter.9.cloned.1.call-start = ((), (), s32[]{:S(2)}) async-start(), calls=%async_computation.11 | async-start | bytes 4718592 | tf_op jit(solution)/shard_map/reduce_scatter | solution.py:43
  363.6 128.6 %reduce-scatter.7.cloned.1.call-start = ((), (), s32[]{:S(2)}) async-start(), calls=%async_computation.9 | async-start | bytes 4718592 | tf_op jit(solution)/shard_map/reduce_scatter | solution.py:43
  420.8 73.3 %copy-start.1 = (bf16[4,2,128,128]{3,2,1,0:T(8,128)(2,1)S(1)}, bf16[4,2,128,128]{3,2,1,0:T(8,128)(2,1)}, u32[]{:S(2)}) copy-start(bf16[4,2,128,128]{3,2,1,0:T(8,128)(2,1)} %param.6) | copy-start | bytes 786436
Sparse Core Ops, SparseCore 0:
  10.1 54.5 all-gather.13
  66.8 51.0 all-gather.7
  120.1 51.0 all-gather.5
  202.6 34.7 reduce-scatter.4
  240.0 53.1 all-gather.9
  315.5 34.6 reduce-scatter.10
  353.0 53.2 all-gather.11
  408.6 35.0 reduce-scatter.8
  446.1 37.3 reduce-scatter.6
where the time goes:
time: 503 us; the launch traced here: 502 us
  waiting for transfers between devices  315 us (63%)
  blocking collectives  65.1 us (13%)
  local copies, waits for them, and re-layouts  50.7 us (10%)
  other arithmetic  38.5 us (8%)
  matrix products  16.3 us (3%)
  between operations  15.7 us (3%)
    all_gather x5, waiting for transfers between devices, product(): gathered = lax.all_gather(right_blocks, 'row', axis=0, tiled=True)  243 us
    reduce_scatter x4, waiting for transfers between devices, product(): lax.psum_scatter(partial_blocks(left_blocks, gathered, targets), 'col', s...  69.7 us
    psum x1, blocking collectives, per_device(): lax.psum(local_trace, ('row', 'col'))  65.1 us
    reduce_sum x3, other arithmetic, partial_blocks(): picked = jnp.where(matched[..., None, None], right_rows[:, :, :, None, :,...  29.8 us
    gather x5, local copies, waits for them, and re-layouts, partial_blocks(): right_rows = gathered[safe_rows]  26.1 us
    dot_general x5, matrix products, partial_blocks(): jnp.einsum('iapr,gisaqr->gispq', left_blocks, picked, preferred_element_t...  16.3 us
    transpose x3, local copies, waits for them, and re-layouts, partial_blocks(): jnp.einsum('iapr,gisaqr->gispq', left_blocks, picked, preferred_element_t...  16.2 us
  transfers between devices with their start and end apart: 9, of which 7 were waited for; matrix products, arithmetic and copies ran while one was open for 9% of the time, Pallas kernels for 0%

commit v1 on v0

--- a/solution.py
+++ b/solution.py
@@ -39,7 +39,14 @@
         return terms.reshape(group_count * row_total, slot_total, block_size, block_size)
 
     def product(left_blocks, right_blocks):
-        gathered = lax.all_gather(right_blocks, "row", axis=0, tiled=True)
+        ring = [right_blocks]
+        for hop in range(15):
+            ring.append(lax.ppermute(ring[-1], "row", [(dev, (dev + 1) % 16) for dev in range(16)]))
+        gathered = jnp.roll(
+            jnp.concatenate(ring[::-1], axis=0),
+            (lax.axis_index("row") + 1) * ring[0].shape[0],
+            axis=0,
+        )
         return lax.psum_scatter(
             partial_blocks(left_blocks, gathered, targets), "col", scatter_dimension=0, tiled=True
         )

time: 503 us -> 873 us (1.74); the launches traced: 502 us -> 863 us
  waiting for transfers between devices: 315 us -> 600 us
  local copies, waits for them, and re-layouts: 50.7 us -> 85.2 us
  blocking collectives: 65.1 us -> 81.6 us
  other arithmetic: 38.5 us -> 53.3 us
  starting transfers between devices: 0.54 us -> 9.32 us
    ppermute x0 -> x75, waiting for transfers between devices: none -> 516 us  [product(): lax.ppermute(ring[-1], 'row', [(dev, (dev + 1) % 16) for dev in range(16)])]
    all_gather x5 -> x0, waiting for transfers between devices: 243 us -> none  [product(): gathered = lax.all_gather(right_blocks, 'row', axis=0, tiled=True)]
    unnamed x13 -> x154, local copies, waits for them, and re-layouts: 1.06 us -> 34.3 us
    psum x1, blocking collectives: 65.1 us -> 81.6 us  [per_device(): lax.psum(local_trace, ('row', 'col'))]
    concatenate x0 -> x5, other arithmetic: none -> 15.8 us  [the longest x4 15.7 us: product(): jnp.roll(jnp.concatenate(ring[::-1], axis=0), (lax.axis_index('row') + 1)...]
    reduce_scatter x4, waiting for transfers between devices: 69.7 us -> 84.2 us  [product(): lax.psum_scatter(partial_blocks(left_blocks, gathered, targets), 'col', s...]
    ppermute x0 -> x75, starting transfers between devices: none -> 9.16 us  [product(): lax.ppermute(ring[-1], 'row', [(dev, (dev + 1) % 16) for dev in range(16)])]
  transfers between devices with their start and end apart: 9 -> 79, of which waited for: 7 -> 75; matrix products, arithmetic and copies ran while one was open for 9% -> 7% of each run, Pallas kernels for 0% -> 0%
where the time goes in v1:
time: 873 us; the launch traced here: 863 us
  waiting for transfers between devices  600 us (69%)
  local copies, waits for them, and re-layouts  85.2 us (10%)
  blocking collectives  81.6 us (9%)
  other arithmetic  53.3 us (6%)
  between operations  16.8 us (2%)
  matrix products  16.6 us (2%)
  starting transfers between devices  9.32 us (1%)
    ppermute x75, waiting for transfers between devices, product(): lax.ppermute(ring[-1], 'row', [(dev, (dev + 1) % 16) for dev in range(16)])  516 us
    reduce_scatter x4, waiting for transfers between devices, product(): lax.psum_scatter(partial_blocks(left_blocks, gathered, targets), 'col', s...  84.2 us
    psum x1, blocking collectives, per_device(): lax.psum(local_trace, ('row', 'col'))  81.6 us
    unnamed x154, local copies, waits for them, and re-layouts  34.3 us
    reduce_sum x3, other arithmetic, partial_blocks(): picked = jnp.where(matched[..., None, None], right_rows[:, :, :, None, :,...  30.1 us
    gather x5, local copies, waits for them, and re-layouts, partial_blocks(): right_rows = gathered[safe_rows]  26.4 us
  transfers between devices with their start and end apart: 79, of which 75 were waited for; matrix products, arithmetic and copies ran while one was open for 7% of the time, Pallas kernels for 0%

profile of v1, /device:TPU:1, one launch (start us, length us, event | category | flops | bytes accessed | tf_op | source)
XLA Modules:
  0.0 862.9 jit_solution(6821174722717358307)
XLA Ops:
  313.2 17.8 %select_reduce_fusion = (bf16[8,4,2,2,128,128]{5,4,3,2,1,0:T(8,128)(2,1)}, bf16[8,4,2,2,128,128]{5,4,3,2,1,0:T(8,128)(2,1)S(1)}, bf16[8,4,2,2,128,128]{5,4,3,2,1,0:T(8,128)(2,1)}) fusion(pred[8,4,2,2,2]{4,3,2,1,0:T(4,128)(4,1)S(1)} %and_and_fusion, bf16[8,4,2,2,128,128]{5,4,3,2,1,0:T(8,128)(2,1)} %bitcast.71, bf16[8,4,2,2,128,128]{5,4,3,2,1,0:T(8,128)(2,1)} %bitcast.72, ...), kind=kLoop, calls=%fused_computation.16 | loop fusion | flops 18874368 | bytes 25166080 | tf_op jit(solution)/shard_map/reduce_sum | solution.py:34
  339.6 34.5 %reduce-scatter.5.cloned.1.call-done = f32[4,2,128,128]{3,2,1,0:T(8,128)} async-done(((f32[32,2,128,128]{3,2,1,0:T(8,128)}), f32[4,2,128,128]{3,2,1,0:T(8,128)}) %reduce-scatter.5.cloned.1.call-update) | async-done | bytes 524304 | tf_op jit(solution)/shard_map/reduce_scatter | solution.py:50
  383.9 8.5 collective-permute-done.31
  392.4 8.5 collective-permute-done.32
  401.0 9.1 %collective-permute-done.33 = bf16[4,2,128,128]{3,2,1,0:T(8,128)(2,1)S(1)} collective-permute-done((bf16[4,2,128,128]{3,2,1,0:T(8,128)(2,1)S(1)}, bf16[4,2,128,128]{3,2,1,0:T(8,128)(2,1)S(1)}, u32[]{:S(2)}, u32[]{:S(2)}) %collective-permute-start.33) | collective-permute-done | bytes 262176 | tf_op jit(solution)/shard_map/ppermute | solution.py:44
  410.1 10.3 %collective-permute-done.34 = bf16[4,2,128,128]{3,2,1,0:T(8,128)(2,1)S(1)} collective-permute-done((bf16[4,2,128,128]{3,2,1,0:T(8,128)(2,1)S(1)}, bf16[4,2,128,128]{3,2,1,0:T(8,128)(2,1)S(1)}, u32[]{:S(2)}, u32[]{:S(2)}) %collective-permute-start.34) | collective-permute-done | bytes 262176 | tf_op jit(solution)/shard_map/ppermute | solution.py:44
  420.4 11.6 %collective-permute-done.35 = bf16[4,2,128,128]{3,2,1,0:T(8,128)(2,1)S(1)} collective-permute-done((bf16[4,2,128,128]{3,2,1,0:T(8,128)(2,1)S(1)}, bf16[4,2,128,128]{3,2,1,0:T(8,128)(2,1)S(1)}, u32[]{:S(2)}, u32[]{:S(2)}) %collective-permute-start.35) | collective-permute-done | bytes 262176 | tf_op jit(solution)/shard_map/ppermute | solution.py:44
  432.0 10.7 %collective-permute-done.36 = bf16[4,2,128,128]{3,2,1,0:T(8,128)(2,1)S(1)} collective-permute-done((bf16[4,2,128,128]{3,2,1,0:T(8,128)(2,1)S(1)}, bf16[4,2,128,128]{3,2,1,0:T(8,128)(2,1)S(1)}, u32[]{:S(2)}, u32[]{:S(2)}) %collective-permute-start.36) | collective-permute-done | bytes 262176 | tf_op jit(solution)/shard_map/ppermute | solution.py:44
  442.7 9.8 %collective-permute-done.37 = bf16[4,2,128,128]{3,2,1,0:T(8,128)(2,1)S(1)} collective-permute-done((bf16[4,2,128,128]{3,2,1,0:T(8,128)(2,1)S(1)}, bf16[4,2,128,128]{3,2,1,0:T(8,128)(2,1)S(1)}, u32[]{:S(2)}, u32[]{:S(2)}) %collective-permute-start.37) | collective-permute-done | bytes 262176 | tf_op jit(solution)/shard_map/ppermute | solution.py:44
  452.5 9.0 %collective-permute-done.38 = bf16[4,2,128,128]{3,2,1,0:T(8,128)(2,1)S(1)} collective-permute-done((bf16[4,2,128,128]{3,2,1,0:T(8,128)(2,1)S(1)}, bf16[4,2,128,128]{3,2,1,0:T(8,128)(2,1)S(1)}, u32[]{:S(2)}, u32[]{:S(2)}) %collective-permute-start.38) | collective-permute-done | bytes 262176 | tf_op jit(solution)/shard_map/ppermute | solution.py:44
  461.5 8.5 collective-permute-done.39
  487.1 8.6 collective-permute-done.42
  495.7 9.8 %collective-permute-done.43 = bf16[4,2,128,128]{3,2,1,0:T(8,128)(2,1)S(1)} collective-permute-done((bf16[4,2,128,128]{3,2,1,0:T(8,128)(2,1)S(1)}, bf16[4,2,128,128]{3,2,1,0:T(8,128)(2,1)S(1)}, u32[]{:S(2)}, u32[]{:S(2)}) %collective-permute-start.43) | collective-permute-done | bytes 262176 | tf_op jit(solution)/shard_map/ppermute | solution.py:44
  505.5 10.9 %collective-permute-done.44 = bf16[4,2,128,128]{3,2,1,0:T(8,128)(2,1)S(1)} collective-permute-done((bf16[4,2,128,128]{3,2,1,0:T(8,128)(2,1)S(1)}, bf16[4,2,128,128]{3,2,1,0:T(8,128)(2,1)S(1)}, u32[]{:S(2)}, u32[]{:S(2)}) %collective-permute-start.44) | collective-permute-done | bytes 262176 | tf_op jit(solution)/shard_map/ppermute | solution.py:44
  542.7 49.7 %reduce-scatter.11.cloned.1.call-done = f32[4,2,128,128]{3,2,1,0:T(8,128)} async-done(((f32[32,2,128,128]{3,2,1,0:T(8,128)}), f32[4,2,128,128]{3,2,1,0:T(8,128)}) %reduce-scatter.11.cloned.1.call-update) | async-done | bytes 524304 | tf_op jit(solution)/shard_map/reduce_scatter | solution.py:50
  631.0 9.1 %collective-permute-done.48 = bf16[4,2,128,128]{3,2,1,0:T(8,128)(2,1)S(1)} collective-permute-done((bf16[4,2,128,128]{3,2,1,0:T(8,128)(2,1)S(1)}, bf16[4,2,128,128]{3,2,1,0:T(8,128)(2,1)S(1)}, u32[]{:S(2)}, u32[]{:S(2)}) %collective-permute-start.48) | collective-permute-done | bytes 262176 | tf_op jit(solution)/shard_map/ppermute | solution.py:44
  640.0 10.2 %collective-permute-done.49 = bf16[4,2,128,128]{3,2,1,0:T(8,128)(2,1)S(1)} collective-permute-done((bf16[4,2,128,128]{3,2,1,0:T(8,128)(2,1)S(1)}, bf16[4,2,128,128]{3,2,1,0:T(8,128)(2,1)S(1)}, u32[]{:S(2)}, u32[]{:S(2)}) %collective-permute-start.49) | collective-permute-done | bytes 262176 | tf_op jit(solution)/shard_map/ppermute | solution.py:44
  650.2 11.6 %collective-permute-done.50 = bf16[4,2,128,128]{3,2,1,0:T(8,128)(2,1)S(1)} collective-permute-done((bf16[4,2,128,128]{3,2,1,0:T(8,128)(2,1)S(1)}, bf16[4,2,128,128]{3,2,1,0:T(8,128)(2,1)S(1)}, u32[]{:S(2)}, u32[]{:S(2)}) %collective-permute-start.50) | collective-permute-done | bytes 262176 | tf_op jit(solution)/shard_map/ppermute | solution.py:44
  661.9 10.8 %collective-permute-done.51 = bf16[4,2,128,128]{3,2,1,0:T(8,128)(2,1)S(1)} collective-permute-done((bf16[4,2,128,128]{3,2,1,0:T(8,128)(2,1)S(1)}, bf16[4,2,128,128]{3,2,1,0:T(8,128)(2,1)S(1)}, u32[]{:S(2)}, u32[]{:S(2)}) %collective-permute-start.51) | collective-permute-done | bytes 262176 | tf_op jit(solution)/shard_map/ppermute | solution.py:44
  672.7 9.9 %collective-permute-done.52 = bf16[4,2,128,128]{3,2,1,0:T(8,128)(2,1)S(1)} collective-permute-done((bf16[4,2,128,128]{3,2,1,0:T(8,128)(2,1)S(1)}, bf16[4,2,128,128]{3,2,1,0:T(8,128)(2,1)S(1)}, u32[]{:S(2)}, u32[]{:S(2)}) %collective-permute-start.52) | collective-permute-done | bytes 262176 | tf_op jit(solution)/shard_map/ppermute | solution.py:44
  682.6 9.1 %collective-permute-done.53 = bf16[4,2,128,128]{3,2,1,0:T(8,128)(2,1)S(1)} collective-permute-done((bf16[4,2,128,128]{3,2,1,0:T(8,128)(2,1)S(1)}, bf16[4,2,128,128]{3,2,1,0:T(8,128)(2,1)S(1)}, u32[]{:S(2)}, u32[]{:S(2)}) %collective-permute-start.53) | collective-permute-done | bytes 262176 | tf_op jit(solution)/shard_map/ppermute | solution.py:44
  726.1 9.7 %collective-permute-done.58 = bf16[4,2,128,128]{3,2,1,0:T(8,128)(2,1)S(1)} collective-permute-done((bf16[4,2,128,128]{3,2,1,0:T(8,128)(2,1)S(1)}, bf16[4,2,128,128]{3,2,1,0:T(8,128)(2,1)S(1)}, u32[]{:S(2)}, u32[]{:S(2)}) %collective-permute-start.58) | collective-permute-done | bytes 262176 | tf_op jit(solution)/shard_map/ppermute | solution.py:44
  735.8 10.8 %collective-permute-done.59 = bf16[4,2,128,128]{3,2,1,0:T(8,128)(2,1)S(1)} collective-permute-done((bf16[4,2,128,128]{3,2,1,0:T(8,128)(2,1)S(1)}, bf16[4,2,128,128]{3,2,1,0:T(8,128)(2,1)S(1)}, u32[]{:S(2)}, u32[]{:S(2)}) %collective-permute-start.59) | collective-permute-done | bytes 262176 | tf_op jit(solution)/shard_map/ppermute | solution.py:44
  770.6 81.6 %psum.7 = f32[]{:T(128)} all-reduce(f32[]{:T(128)} %get-tuple-element.6), channel_id=1, replica_groups=mesh['row'=16,'col'=8] {'row','col'}, use_global_device_ids=true, to_apply=%region_11.13 | all-reduce | flops 1 | bytes 8 | tf_op jit(solution)/shard_map/psum | solution.py:58
  (337 shorter events, 466.0 us)
Async XLA Ops:
  7.2 366.9 %reduce-scatter.5.cloned.1.call-start = ((), (), s32[]{:S(2)}) async-start(), calls=%async_computation.4 | async-start | bytes 4718592 | tf_op jit(solution)/shard_map/reduce_scatter | solution.py:50
  11.4 20.4 %collective-permute-start.60 = (bf16[4,2,128,128]{3,2,1,0:T(8,128)(2,1)}, bf16[4,2,128,128]{3,2,1,0:T(8,128)(2,1)S(1)}, u32[]{:S(2)}, u32[]{:S(2)}) collective-permute-start(bf16[4,2,128,128]{3,2,1,0:T(8,128)(2,1)} %param.11), channel_id=1, source_target_pairs={{0,8},{8,16},{16,24},{24,32},{32,40},{40,48},{48,56},{56,64},{64,7... | collective-permute-start | bytes 786440 | tf_op jit(solution)/shard_map/ppermute | solution.py:44
  20.5 16.9 %collective-permute-start.1 = (bf16[4,2,128,128]{3,2,1,0:T(8,128)(2,1)S(1)}, bf16[4,2,128,128]{3,2,1,0:T(8,128)(2,1)S(1)}, u32[]{:S(2)}, u32[]{:S(2)}) collective-permute-start(bf16[4,2,128,128]{3,2,1,0:T(8,128)(2,1)S(1)} %collective-permute-done), channel_id=1, source_target_pairs={{0,8},{8,16},{16,24},{24,32},{32,40},{40,48},{48,56},{56,64},{64,7... | collective-permute-start | bytes 786440 | tf_op jit(solution)/shard_map/ppermute | solution.py:44
  26.2 16.9 %collective-permute-start.16 = (bf16[4,2,128,128]{3,2,1,0:T(8,128)(2,1)S(1)}, bf16[4,2,128,128]{3,2,1,0:T(8,128)(2,1)S(1)}, u32[]{:S(2)}, u32[]{:S(2)}) collective-permute-start(bf16[4,2,128,128]{3,2,1,0:T(8,128)(2,1)S(1)} %collective-permute-done.15), channel_id=1, source_target_pairs={{0,8},{8,16},{16,24},{24,32},{32,40},{40,48},{48,56},{56,64},{64,7... | collective-permute-start | bytes 786440 | tf_op jit(solution)/shard_map/ppermute | solution.py:44
  31.8 16.9 %collective-permute-start.61 = (bf16[4,2,128,128]{3,2,1,0:T(8,128)(2,1)S(1)}, bf16[4,2,128,128]{3,2,1,0:T(8,128)(2,1)S(1)}, u32[]{:S(2)}, u32[]{:S(2)}) collective-permute-start(bf16[4,2,128,128]{3,2,1,0:T(8,128)(2,1)S(1)} %collective-permute-done.60), channel_id=1, source_target_pairs={{0,8},{8,16},{16,24},{24,32},{32,40},{40,48},{48,56},{56,64},{64,7... | collective-permute-start | bytes 786440 | tf_op jit(solution)/shard_map/ppermute | solution.py:44
  37.4 16.9 %collective-permute-start.2 = (bf16[4,2,128,128]{3,2,1,0:T(8,128)(2,1)S(1)}, bf16[4,2,128,128]{3,2,1,0:T(8,128)(2,1)S(1)}, u32[]{:S(2)}, u32[]{:S(2)}) collective-permute-start(bf16[4,2,128,128]{3,2,1,0:T(8,128)(2,1)S(1)} %collective-permute-done.1), channel_id=1, source_target_pairs={{0,8},{8,16},{16,24},{24,32},{32,40},{40,48},{48,56},{56,64},{64,7... | collective-permute-start | bytes 786440 | tf_op jit(solution)/shard_map/ppermute | solution.py:44
  48.6 16.9 %collective-permute-start.62 = (bf16[4,2,128,128]{3,2,1,0:T(8,128)(2,1)S(1)}, bf16[4,2,128,128]{3,2,1,0:T(8,128)(2,1)S(1)}, u32[]{:S(2)}, u32[]{:S(2)}) collective-permute-start(bf16[4,2,128,128]{3,2,1,0:T(8,128)(2,1)S(1)} %collective-permute-done.61), channel_id=1, source_target_pairs={{0,8},{8,16},{16,24},{24,32},{32,40},{40,48},{48,56},{56,64},{64,7... | collective-permute-start | bytes 786440 | tf_op jit(solution)/shard_map/ppermute | solution.py:44
  59.9 16.9 %collective-permute-start.18 = (bf16[4,2,128,128]{3,2,1,0:T(8,128)(2,1)S(1)}, bf16[4,2,128,128]{3,2,1,0:T(8,128)(2,1)S(1)}, u32[]{:S(2)}, u32[]{:S(2)}) collective-permute-start(bf16[4,2,128,128]{3,2,1,0:T(8,128)(2,1)S(1)} %collective-permute-done.17), channel_id=1, source_target_pairs={{0,8},{8,16},{16,24},{24,32},{32,40},{40,48},{48,56},{56,64},{64,7... | collective-permute-start | bytes 786440 | tf_op jit(solution)/shard_map/ppermute | solution.py:44
  65.5 16.9 %collective-permute-start.63 = (bf16[4,2,128,128]{3,2,1,0:T(8,128)(2,1)S(1)}, bf16[4,2,128,128]{3,2,1,0:T(8,128)(2,1)S(1)}, u32[]{:S(2)}, u32[]{:S(2)}) collective-permute-start(bf16[4,2,128,128]{3,2,1,0:T(8,128)(2,1)S(1)} %collective-permute-done.62), channel_id=1, source_target_pairs={{0,8},{8,16},{16,24},{24,32},{32,40},{40,48},{48,56},{56,64},{64,7... | collective-permute-start | bytes 786440 | tf_op jit(solution)/shard_map/ppermute | solution.py:44
  76.7 16.9 %collective-permute-start.19 = (bf16[4,2,128,128]{3,2,1,0:T(8,128)(2,1)S(1)}, bf16[4,2,128,128]{3,2,1,0:T(8,128)(2,1)S(1)}, u32[]{:S(2)}, u32[]{:S(2)}) collective-permute-start(bf16[4,2,128,128]{3,2,1,0:T(8,128)(2,1)S(1)} %collective-permute-done.18), channel_id=1, source_target_pairs={{0,8},{8,16},{16,24},{24,32},{32,40},{40,48},{48,56},{56,64},{64,7... | collective-permute-start | bytes 786440 | tf_op jit(solution)/shard_map/ppermute | solution.py:44
  166.6 17.0 %collective-permute-start.69 = (bf16[4,2,128,128]{3,2,1,0:T(8,128)(2,1)S(1)}, bf16[4,2,128,128]{3,2,1,0:T(8,128)(2,1)}, u32[]{:S(2)}, u32[]{:S(2)}) collective-permute-start(bf16[4,2,128,128]{3,2,1,0:T(8,128)(2,1)S(1)} %collective-permute-done.68), channel_id=1, source_target_pairs={{0,8},{8,16},{16,24},{24,32},{32,40},{40,48},{48,56},{56,64},{64,7... | collective-permute-start | bytes 786440 | tf_op jit(solution)/shard_map/ppermute | solution.py:44
  172.2 17.0 %collective-permute-start.10 = (bf16[4,2,128,128]{3,2,1,0:T(8,128)(2,1)S(1)}, bf16[4,2,128,128]{3,2,1,0:T(8,128)(2,1)}, u32[]{:S(2)}, u32[]{:S(2)}) collective-permute-start(bf16[4,2,128,128]{3,2,1,0:T(8,128)(2,1)S(1)} %collective-permute-done.9), channel_id=1, source_target_pairs={{0,8},{8,16},{16,24},{24,32},{32,40},{40,48},{48,56},{56,64},{64,7... | collective-permute-start | bytes 786440 | tf_op jit(solution)/shard_map/ppermute | solution.py:44
  177.8 17.0 %collective-permute-start.25 = (bf16[4,2,128,128]{3,2,1,0:T(8,128)(2,1)S(1)}, bf16[4,2,128,128]{3,2,1,0:T(8,128)(2,1)}, u32[]{:S(2)}, u32[]{:S(2)}) collective-permute-start(bf16[4,2,128,128]{3,2,1,0:T(8,128)(2,1)S(1)} %collective-permute-done.24), channel_id=1, source_target_pairs={{0,8},{8,16},{16,24},{24,32},{32,40},{40,48},{48,56},{56,64},{64,7... | collective-permute-start | bytes 786440 | tf_op jit(solution)/shard_map/ppermute | solution.py:44
  194.8 16.9 %collective-permute-start.26 = (bf16[4,2,128,128]{3,2,1,0:T(8,128)(2,1)}, bf16[4,2,128,128]{3,2,1,0:T(8,128)(2,1)}, u32[]{:S(2)}, u32[]{:S(2)}) collective-permute-start(bf16[4,2,128,128]{3,2,1,0:T(8,128)(2,1)} %collective-permute-done.25), channel_id=1, source_target_pairs={{0,8},{8,16},{16,24},{24,32},{32,40},{40,48},{48,56},{56,64},{64,7... | collective-permute-start | bytes 786440 | tf_op jit(solution)/shard_map/ppermute | solution.py:44
  206.0 16.9 %collective-permute-start.12 = (bf16[4,2,128,128]{3,2,1,0:T(8,128)(2,1)}, bf16[4,2,128,128]{3,2,1,0:T(8,128)(2,1)}, u32[]{:S(2)}, u32[]{:S(2)}) collective-permute-start(bf16[4,2,128,128]{3,2,1,0:T(8,128)(2,1)} %collective-permute-done.11), channel_id=1, source_target_pairs={{0,8},{8,16},{16,24},{24,32},{32,40},{40,48},{48,56},{56,64},{64,7... | collective-permute-start | bytes 786440 | tf_op jit(solution)/shard_map/ppermute | solution.py:44
  211.7 16.9 %collective-permute-start.27 = (bf16[4,2,128,128]{3,2,1,0:T(8,128)(2,1)}, bf16[4,2,128,128]{3,2,1,0:T(8,128)(2,1)}, u32[]{:S(2)}, u32[]{:S(2)}) collective-permute-start(bf16[4,2,128,128]{3,2,1,0:T(8,128)(2,1)} %collective-permute-done.26), channel_id=1, source_target_pairs={{0,8},{8,16},{16,24},{24,32},{32,40},{40,48},{48,56},{56,64},{64,7... | collective-permute-start | bytes 786440 | tf_op jit(solution)/shard_map/ppermute | solution.py:44
  222.9 16.9 %collective-permute-start.13 = (bf16[4,2,128,128]{3,2,1,0:T(8,128)(2,1)}, bf16[4,2,128,128]{3,2,1,0:T(8,128)(2,1)}, u32[]{:S(2)}, u32[]{:S(2)}) collective-permute-start(bf16[4,2,128,128]{3,2,1,0:T(8,128)(2,1)} %collective-permute-done.12), channel_id=1, source_target_pairs={{0,8},{8,16},{16,24},{24,32},{32,40},{40,48},{48,56},{56,64},{64,7... | collective-permute-start | bytes 786440 | tf_op jit(solution)/shard_map/ppermute | solution.py:44
  234.1 16.9 %collective-permute-start.73 = (bf16[4,2,128,128]{3,2,1,0:T(8,128)(2,1)}, bf16[4,2,128,128]{3,2,1,0:T(8,128)(2,1)}, u32[]{:S(2)}, u32[]{:S(2)}) collective-permute-start(bf16[4,2,128,128]{3,2,1,0:T(8,128)(2,1)} %collective-permute-done.72), channel_id=1, source_target_pairs={{0,8},{8,16},{16,24},{24,32},{32,40},{40,48},{48,56},{56,64},{64,7... | collective-permute-start | bytes 786440 | tf_op jit(solution)/shard_map/ppermute | solution.py:44
  239.7 16.9 %collective-permute-start.14 = (bf16[4,2,128,128]{3,2,1,0:T(8,128)(2,1)}, bf16[4,2,128,128]{3,2,1,0:T(8,128)(2,1)}, u32[]{:S(2)}, u32[]{:S(2)}) collective-permute-start(bf16[4,2,128,128]{3,2,1,0:T(8,128)(2,1)} %collective-permute-done.13), channel_id=1, source_target_pairs={{0,8},{8,16},{16,24},{24,32},{32,40},{40,48},{48,56},{56,64},{64,7... | collective-permute-start | bytes 786440 | tf_op jit(solution)/shard_map/ppermute | solution.py:44
  245.4 44.3 %collective-permute-start.29 = (bf16[4,2,128,128]{3,2,1,0:T(8,128)(2,1)}, bf16[4,2,128,128]{3,2,1,0:T(8,128)(2,1)}, u32[]{:S(2)}, u32[]{:S(2)}) collective-permute-start(bf16[4,2,128,128]{3,2,1,0:T(8,128)(2,1)} %collective-permute-done.28), channel_id=1, source_target_pairs={{0,8},{8,16},{16,24},{24,32},{32,40},{40,48},{48,56},{56,64},{64,7... | collective-permute-start | bytes 786440 | tf_op jit(solution)/shard_map/ppermute | solution.py:44
  251.0 16.9 %collective-permute-start.74 = (bf16[4,2,128,128]{3,2,1,0:T(8,128)(2,1)}, bf16[4,2,128,128]{3,2,1,0:T(8,128)(2,1)S(1)}, u32[]{:S(2)}, u32[]{:S(2)}) collective-permute-start(bf16[4,2,128,128]{3,2,1,0:T(8,128)(2,1)} %collective-permute-done.73), channel_id=1, source_target_pairs={{0,8},{8,16},{16,24},{24,32},{32,40},{40,48},{48,56},{56,64},{64,7... | collective-permute-start | bytes 786440 | tf_op jit(solution)/shard_map/ppermute | solution.py:44
  339.6 252.9 %reduce-scatter.11.cloned.1.call-start = ((), (), s32[]{:S(2)}) async-start(), calls=%async_computation.7 | async-start | bytes 4718592 | tf_op jit(solution)/shard_map/reduce_scatter | solution.py:50
  542.7 310.2 %reduce-scatter.9.cloned.1.call-start = ((), (), s32[]{:S(2)}) async-start(), calls=%async_computation.6 | async-start | bytes 4718592 | tf_op jit(solution)/shard_map/reduce_scatter | solution.py:50
  605.1 247.7 %reduce-scatter.7.cloned.1.call-start = ((), (), s32[]{:S(2)}) async-start(), calls=%async_computation.5 | async-start | bytes 4718592 | tf_op jit(solution)/shard_map/reduce_scatter | solution.py:50
  (94 other events, 2127.0 us)
Sparse Core Ops, SparseCore 0:
  339.7 34.3 reduce-scatter.4
  542.8 49.6 reduce-scatter.10
  605.3 36.9 reduce-scatter.8
  770.7 50.0 reduce-scatter.6
